TPU v7x, 32 devices: a whole 2x2x4 slice. The times are simulated.
32 devices in a mesh: freq: 2 (over y), slab: 16 (over z, x, core).
Axes of the slice: x: 2, y: 2, z: 4, core: 2. Of those that a mesh axis runs over, the one named last changes fastest.
Arguments:
- wavefield: float32 [2, 2, 2048, 2048], P(None, 'freq', 'slab'), may hold values from -6 to 6
- freqs: float32 [2], P('freq'), may hold values from 0.15 to 0.45
- velocity: float32 [3, 2048, 2048], P(None, 'slab', 'freq'), may hold values from 0.7 to 1.6
- ref_slow: float32 [3, 2], replicated, may hold values from 0.6 to 1.5, as said below
Outputs:
- migrated: float32 [2, 2, 2048, 2048], P(None, 'freq', 'slab')
Inputs may be any that keep to these rules, and one draw needn't show every extreme that they name: ref_slow[d, 1] - ref_slow[d, 0] lies between 0.3 and 0.6 for every depth step.
All inputs are finite; a program needn't handle non-finite values.
Results may differ from a plain program's by a relative error of at most 0.0003.
Values sent between devices are 32-bit elements; how exact they have to be, the bound alone decides.
A program may use at most 64 MiB of HBM per device.

v0:
```python
import math
import jax
import jax.numpy as jnp
from jax import lax
from jax.sharding import PartitionSpec as P

two_pi = 2.0 * math.pi
depth_step = 2.0


def dft_matrix(length, sign):
    index = jnp.arange(length, dtype=jnp.int32)
    product = index[:, None] * index[None, :] % length
    angle = sign * two_pi / length * product.astype(jnp.float32)
    scale = 1.0 / math.sqrt(length)
    return (jnp.cos(angle) * scale, jnp.sin(angle) * scale)


def twiddle(outer, inner, sign):
    length = outer * inner
    product = (
        jnp.arange(outer, dtype=jnp.int32)[:, None]
        * jnp.arange(inner, dtype=jnp.int32)[None, :]
        % length
    )
    angle = sign * two_pi / length * product.astype(jnp.float32)
    return (jnp.cos(angle), jnp.sin(angle))


def complex_mix(form, mat_real, mat_imag, data_real, data_imag):

    def product(matrix, data):
        return jnp.einsum(form, matrix, data, precision=lax.Precision.HIGHEST)

    return (
        product(mat_real, data_real) - product(mat_imag, data_imag),
        product(mat_real, data_imag) + product(mat_imag, data_real),
    )


def transform(real, imag, trailing, sign):
    length = real.shape[-2] if trailing else real.shape[-1]
    inner = min(length, 128)
    outer = length // inner
    outer_real, outer_imag = dft_matrix(outer, sign)
    inner_real, inner_imag = dft_matrix(inner, sign)
    turn_real, turn_imag = twiddle(outer, inner, sign)
    if trailing:
        leading = real.shape[:-2]
        tail = real.shape[-1:]
        form_outer = "ka,...abm->...kbm"
        form_inner = "bj,...kbm->...kjm"
        turn_real = turn_real[:, :, None]
        turn_imag = turn_imag[:, :, None]
    else:
        leading = real.shape[:-1]
        tail = ()
        form_outer = "ka,...ab->...kb"
        form_inner = "bj,...kb->...kj"
    split_shape = leading + (outer, inner) + tail
    real = real.reshape(split_shape)
    imag = imag.reshape(split_shape)
    if sign < 0:
        real, imag = complex_mix(form_outer, outer_real, outer_imag, real, imag)
        real, imag = (real * turn_real - imag * turn_imag, real * turn_imag + imag * turn_real)
        real, imag = complex_mix(form_inner, inner_real, inner_imag, real, imag)
    else:
        real, imag = complex_mix(form_inner, inner_real, inner_imag, real, imag)
        real, imag = (real * turn_real - imag * turn_imag, real * turn_imag + imag * turn_real)
        real, imag = complex_mix(form_outer, outer_real, outer_imag, real, imag)
    joined = leading + (length,) + tail
    return (real.reshape(joined), imag.reshape(joined))


def wave_numbers(positions, length):
    inner = min(length, 128)
    outer = length // inner
    number = positions // inner + outer * (positions % inner)
    number = jnp.where(number < length // 2, number, number - length)
    return number.astype(jnp.float32) / length


def forward_x(items):
    real, imag = transform(items[0], items[1], True, -1)
    return jnp.stack((real, imag))


def inverse_y(items):
    real, imag = transform(items[:, 0], items[:, 1], False, 1)
    return jnp.stack((real, imag), axis=1)


def shards(wavefield, freqs, velocity, ref_slow):
    slabs = lax.axis_size("slab")
    slab_index = lax.axis_index("slab")
    rows = wavefield.shape[2]
    width_x = rows * slabs
    width_y = wavefield.shape[3]
    columns = width_y // slabs
    depth = ref_slow.shape[0]
    along_x = wave_numbers(jnp.arange(width_x, dtype=jnp.int32), width_x)
    along_y = wave_numbers(slab_index * columns + jnp.arange(columns, dtype=jnp.int32), width_y)
    square = along_x[:, None] ** 2 + along_y[None, :] ** 2
    freq_col = freqs[:, None, None]

    def advance(level, field):
        local_tile = lax.dynamic_index_in_dim(velocity, level, 0, keepdims=False)
        tile = lax.all_gather(local_tile, "freq", axis=1, tiled=True)
        real, imag = transform(field[0], field[1], False, -1)
        spectrum = forward_x(
            lax.all_to_all(jnp.stack((real, imag)), "slab", split_axis=3, concat_axis=2, tiled=True)
        )
        slow_pair = lax.dynamic_index_in_dim(ref_slow, level, 0, keepdims=False)
        slowness = 1.0 / tile
        upper_weight = jnp.clip((slowness - slow_pair[0]) / (slow_pair[1] - slow_pair[0]), 0.0, 1.0)
        weights = [1.0 - upper_weight, upper_weight]
        shifted = []
        for branch in range(2):
            target = (freq_col * slow_pair[branch]) ** 2 - square[None]
            angle = two_pi * depth_step * jnp.sqrt(jnp.abs(target))
            live = target >= 0
            prop_real = jnp.where(live, jnp.cos(angle), jnp.exp(-angle))
            prop_imag = jnp.where(live, jnp.sin(angle), jnp.zeros_like(angle))
            spec_real = spectrum[0] * prop_real - spectrum[1] * prop_imag
            spec_imag = spectrum[0] * prop_imag + spectrum[1] * prop_real
            back_real, back_imag = transform(spec_real, spec_imag, True, 1)
            shifted.append(jnp.stack((back_real, back_imag)))
        pieces = []
        for branch in range(2):
            moved = lax.all_to_all(shifted[branch], "slab", split_axis=2, concat_axis=3, tiled=True)
            pieces.append(inverse_y(moved[None])[0])
        spatial = jnp.stack(pieces)
        new_real = jnp.zeros_like(field[0])
        new_imag = jnp.zeros_like(field[1])
        for branch in range(2):
            theta = two_pi * depth_step * freq_col * (slowness - slow_pair[branch])[None]
            weight = weights[branch][None]
            cosine = jnp.cos(theta)
            sine = jnp.sin(theta)
            part_real = spatial[branch, 0]
            part_imag = spatial[branch, 1]
            new_real = new_real + weight * (cosine * part_real - sine * part_imag)
            new_imag = new_imag + weight * (cosine * part_imag + sine * part_real)
        return jnp.stack((new_real, new_imag))

    return lax.fori_loop(0, depth, advance, wavefield)


def solution(mesh):
    return jax.shard_map(
        shards,
        mesh=mesh,
        in_specs=(P(None, "freq", "slab", None), P("freq"), P(None, "slab", "freq"), P()),
        out_specs=P(None, "freq", "slab", None),
        check_vma=False,
    )
```

profile of v0, /device:TPU:11, one launch (start us, length us, event | category | flops | bytes accessed | tf_op | source)
XLA Modules:
  0.0 790.6 jit_solution(8718204456309350147)
XLA Ops:
  8.1 774.4 %while.17 = (s32[]{:T(128)}, f32[2,1,128,2048]{3,2,1,0:T(8,128)S(1)}, f32[3,128,1024]{2,1,0:T(8,128)}, f32[3,2]{0,1:T(2,128)S(1)}, f32[1,1,1]{2,1,0:T(1,128)}, /...) while((s32[]{:T(128)}, f32[2,1,128,2048]{3,2,1,0:T(8,128)S(1)}, ...), condition=%wide.region_1.2_spmd.clone, body=%wide.region_0.1_spmd.clone.sunk | while | flops 10909407232 | bytes 317449280 | solution.py:146
  23.0 6.5 all-to-all-start
  32.9 10.2 %fusion.669 = (f32[2048,128]{1,0:T(8,128)}, f32[2048,128]{1,0:T(8,128)}, f32[2048,128]{1,0:T(8,128)S(1)}, f32[2048,128]{1,0:T(8,128)}) fusion(f32[128]{0:T(128)S(1)} %get-tuple-element.413, f32[2048]{0:T(1024)S(1)} %get-tuple-element.414, f32[]{:T(128)} %bitcast.650, f32[]{:T(128)} %bitcast.652), kind=kLoop, calls=%fused_computation.62.clone.1 | loop fusion | flops 3932160 | bytes 4203016 | tf_op jit(solution)/shard_map/while/body/eval_jaxpr/jit(_where)/select_n | solution.py:123
  52.1 24.8 %all-to-all-done = f32[2,1,128,2048]{2,1,0,3:T(1,128)S(1)} async-done(((f32[2,1,128,2048]{2,1,0,3:T(1,128)}), f32[2,1,128,2048]{2,1,0,3:T(1,128)S(1)}, u32[]{:S(2)}, u32[]{:S(2)}) %all-to-all-start) | async-done | bytes 2097184 | tf_op jit(solution)/shard_map/while/body/eval_jaxpr/all_to_all | solution.py:111
  114.7 10.2 %copy.403 = f32[2,1,2048,128]{3,1,0,2:T(1,128)} copy(f32[2,1,2048,128]{3,2,1,0:T(8,128)S(1)} %pad_maximum_fusion.10) | data formatting | bytes 4194304 | tf_op jit(solution)/shard_map/while/body/eval_jaxpr/stack | solution.py:127
  124.9 4.9 all-to-all-start.2
  136.0 10.0 %copy.396 = f32[2,1,2048,128]{3,1,0,2:T(1,128)} copy(f32[2,1,2048,128]{3,2,1,0:T(8,128)S(1)} %pad_maximum_fusion.9) | data formatting | bytes 4194304 | tf_op jit(solution)/shard_map/while/body/eval_jaxpr/stack | solution.py:127
  145.9 31.4 %all-to-all-done.2 = f32[2,1,2048,128]{3,1,0,2:T(1,128)} async-done(((f32[2,1,2048,128]{3,1,0,2:T(1,128)}), f32[2,1,2048,128]{3,1,0,2:T(1,128)}, u32[]{:S(2)}, u32[]{:S(2)}) %all-to-all-start.2) | async-done | bytes 2097184 | tf_op jit(solution)/shard_map/while/body/eval_jaxpr/all_to_all | solution.py:130
  177.3 4.8 all-to-all-start.1
  202.3 27.2 %all-to-all-done.1 = f32[2,1,2048,128]{3,1,0,2:T(1,128)S(1)} async-done(((f32[2,1,2048,128]{3,1,0,2:T(1,128)}), f32[2,1,2048,128]{3,1,0,2:T(1,128)S(1)}, u32[]{:S(2)}, u32[]{:S(2)}) %all-to-all-start.1) | async-done | bytes 2097184 | tf_op jit(solution)/shard_map/while/body/eval_jaxpr/all_to_all | solution.py:130
  255.7 10.9 %fusion.706 = (f32[1,1,128,2048]{3,2,1,0:T(8,128)S(1)}, f32[1,1,128,2048]{3,2,1,0:T(8,128)S(1)}) fusion(f32[16,8,16,128]{3,2,1,0:T(8,128)} %bitcast.711, f32[16,8,16,128]{3,2,1,0:T(8,128)S(1)} %bitcast.710, f32[16,8,16,128]{3,2,1,0:T(8,128)S(1)} %bitcast.709, f32[16,8,16,128]{3,2,1,0:T(8,128)S(1)} %bitcast.708, f32[]{:T(128)} %bitcast.679, ...), kind=kLoop, calls=%fused_computation.70.clone.1 | loop fusion | flops 6815744 | bytes 7340048 | tf_op jit(solution)/shard_map/while/body/eval_jaxpr/stack | solution.py:144
  282.0 4.8 all-to-all-start
  290.1 10.2 %fusion.669 = (f32[2048,128]{1,0:T(8,128)}, f32[2048,128]{1,0:T(8,128)}, f32[2048,128]{1,0:T(8,128)S(1)}, f32[2048,128]{1,0:T(8,128)}) fusion(f32[128]{0:T(128)S(1)} %get-tuple-element.413, f32[2048]{0:T(1024)S(1)} %get-tuple-element.414, f32[]{:T(128)} %bitcast.650, f32[]{:T(128)} %bitcast.652), kind=kLoop, calls=%fused_computation.62.clone.1 | loop fusion | flops 3932160 | bytes 4203016 | tf_op jit(solution)/shard_map/while/body/eval_jaxpr/jit(_where)/select_n | solution.py:123
  309.3 24.8 %all-to-all-done = f32[2,1,128,2048]{2,1,0,3:T(1,128)S(1)} async-done(((f32[2,1,128,2048]{2,1,0,3:T(1,128)}), f32[2,1,128,2048]{2,1,0,3:T(1,128)S(1)}, u32[]{:S(2)}, u32[]{:S(2)}) %all-to-all-start) | async-done | bytes 2097184 | tf_op jit(solution)/shard_map/while/body/eval_jaxpr/all_to_all | solution.py:111
  371.8 10.2 %copy.403 = f32[2,1,2048,128]{3,1,0,2:T(1,128)} copy(f32[2,1,2048,128]{3,2,1,0:T(8,128)S(1)} %pad_maximum_fusion.10) | data formatting | bytes 4194304 | tf_op jit(solution)/shard_map/while/body/eval_jaxpr/stack | solution.py:127
  382.0 4.9 all-to-all-start.2
  393.0 10.0 %copy.396 = f32[2,1,2048,128]{3,1,0,2:T(1,128)} copy(f32[2,1,2048,128]{3,2,1,0:T(8,128)S(1)} %pad_maximum_fusion.9) | data formatting | bytes 4194304 | tf_op jit(solution)/shard_map/while/body/eval_jaxpr/stack | solution.py:127
  403.0 31.4 %all-to-all-done.2 = f32[2,1,2048,128]{3,1,0,2:T(1,128)} async-done(((f32[2,1,2048,128]{3,1,0,2:T(1,128)}), f32[2,1,2048,128]{3,1,0,2:T(1,128)}, u32[]{:S(2)}, u32[]{:S(2)}) %all-to-all-start.2) | async-done | bytes 2097184 | tf_op jit(solution)/shard_map/while/body/eval_jaxpr/all_to_all | solution.py:130
  434.4 4.8 all-to-all-start.1
  459.2 27.4 %all-to-all-done.1 = f32[2,1,2048,128]{3,1,0,2:T(1,128)S(1)} async-done(((f32[2,1,2048,128]{3,1,0,2:T(1,128)}), f32[2,1,2048,128]{3,1,0,2:T(1,128)S(1)}, u32[]{:S(2)}, u32[]{:S(2)}) %all-to-all-start.1) | async-done | bytes 2097184 | tf_op jit(solution)/shard_map/while/body/eval_jaxpr/all_to_all | solution.py:130
  513.0 10.9 %fusion.706 = (f32[1,1,128,2048]{3,2,1,0:T(8,128)S(1)}, f32[1,1,128,2048]{3,2,1,0:T(8,128)S(1)}) fusion(f32[16,8,16,128]{3,2,1,0:T(8,128)} %bitcast.711, f32[16,8,16,128]{3,2,1,0:T(8,128)S(1)} %bitcast.710, f32[16,8,16,128]{3,2,1,0:T(8,128)S(1)} %bitcast.709, f32[16,8,16,128]{3,2,1,0:T(8,128)S(1)} %bitcast.708, f32[]{:T(128)} %bitcast.679, ...), kind=kLoop, calls=%fused_computation.70.clone.1 | loop fusion | flops 6815744 | bytes 7340048 | tf_op jit(solution)/shard_map/while/body/eval_jaxpr/stack | solution.py:144
  535.8 3.4 pad_maximum_fusion.8
  539.3 4.8 all-to-all-start
  547.4 10.2 %fusion.669 = (f32[2048,128]{1,0:T(8,128)}, f32[2048,128]{1,0:T(8,128)}, f32[2048,128]{1,0:T(8,128)S(1)}, f32[2048,128]{1,0:T(8,128)}) fusion(f32[128]{0:T(128)S(1)} %get-tuple-element.413, f32[2048]{0:T(1024)S(1)} %get-tuple-element.414, f32[]{:T(128)} %bitcast.650, f32[]{:T(128)} %bitcast.652), kind=kLoop, calls=%fused_computation.62.clone.1 | loop fusion | flops 3932160 | bytes 4203016 | tf_op jit(solution)/shard_map/while/body/eval_jaxpr/jit(_where)/select_n | solution.py:123
  566.6 24.8 %all-to-all-done = f32[2,1,128,2048]{2,1,0,3:T(1,128)S(1)} async-done(((f32[2,1,128,2048]{2,1,0,3:T(1,128)}), f32[2,1,128,2048]{2,1,0,3:T(1,128)S(1)}, u32[]{:S(2)}, u32[]{:S(2)}) %all-to-all-start) | async-done | bytes 2097184 | tf_op jit(solution)/shard_map/while/body/eval_jaxpr/all_to_all | solution.py:111
  628.9 10.4 %copy.403 = f32[2,1,2048,128]{3,1,0,2:T(1,128)} copy(f32[2,1,2048,128]{3,2,1,0:T(8,128)S(1)} %pad_maximum_fusion.10) | data formatting | bytes 4194304 | tf_op jit(solution)/shard_map/while/body/eval_jaxpr/stack | solution.py:127
  639.3 4.9 all-to-all-start.2
  650.3 10.0 %copy.396 = f32[2,1,2048,128]{3,1,0,2:T(1,128)} copy(f32[2,1,2048,128]{3,2,1,0:T(8,128)S(1)} %pad_maximum_fusion.9) | data formatting | bytes 4194304 | tf_op jit(solution)/shard_map/while/body/eval_jaxpr/stack | solution.py:127
  660.3 31.4 %all-to-all-done.2 = f32[2,1,2048,128]{3,1,0,2:T(1,128)} async-done(((f32[2,1,2048,128]{3,1,0,2:T(1,128)}), f32[2,1,2048,128]{3,1,0,2:T(1,128)}, u32[]{:S(2)}, u32[]{:S(2)}) %all-to-all-start.2) | async-done | bytes 2097184 | tf_op jit(solution)/shard_map/while/body/eval_jaxpr/all_to_all | solution.py:130
  691.7 4.8 all-to-all-start.1
  716.4 27.5 %all-to-all-done.1 = f32[2,1,2048,128]{3,1,0,2:T(1,128)S(1)} async-done(((f32[2,1,2048,128]{3,1,0,2:T(1,128)}), f32[2,1,2048,128]{3,1,0,2:T(1,128)S(1)}, u32[]{:S(2)}, u32[]{:S(2)}) %all-to-all-start.1) | async-done | bytes 2097184 | tf_op jit(solution)/shard_map/while/body/eval_jaxpr/all_to_all | solution.py:130
  770.3 10.9 %fusion.706 = (f32[1,1,128,2048]{3,2,1,0:T(8,128)S(1)}, f32[1,1,128,2048]{3,2,1,0:T(8,128)S(1)}) fusion(f32[16,8,16,128]{3,2,1,0:T(8,128)} %bitcast.711, f32[16,8,16,128]{3,2,1,0:T(8,128)S(1)} %bitcast.710, f32[16,8,16,128]{3,2,1,0:T(8,128)S(1)} %bitcast.709, f32[16,8,16,128]{3,2,1,0:T(8,128)S(1)} %bitcast.708, f32[]{:T(128)} %bitcast.679, ...), kind=kLoop, calls=%fused_computation.70.clone.1 | loop fusion | flops 6815744 | bytes 7340048 | tf_op jit(solution)/shard_map/while/body/eval_jaxpr/stack | solution.py:144
  (316 shorter events, 338.5 us)
Async XLA Ops:
  6.5 1.6 copy-start.9
  6.5 1.6 copy-start.10
  23.0 53.9 %all-to-all-start = ((f32[2,1,128,2048]{2,1,0,3:T(1,128)}), f32[2,1,128,2048]{2,1,0,3:T(1,128)S(1)}, u32[]{:S(2)}, u32[]{:S(2)}) async-start(f32[2,1,128,2048]{2,1,0,3:T(1,128)} %pad_maximum_fusion.8), calls=%async_computation | async-start | bytes 4194304 | tf_op jit(solution)/shard_map/while/body/eval_jaxpr/all_to_all | solution.py:111
  76.9 1.3 copy-start
  89.8 2.5 copy-start.7
  91.1 1.5 copy-start.5
  91.1 1.8 copy-start.6
  124.9 4.9 copy-start.2
  124.9 52.4 %all-to-all-start.2 = ((f32[2,1,2048,128]{3,1,0,2:T(1,128)}), f32[2,1,2048,128]{3,1,0,2:T(1,128)}, u32[]{:S(2)}, u32[]{:S(2)}) async-start(f32[2,1,2048,128]{3,1,0,2:T(1,128)} %copy.403), calls=%async_computation.2 | async-start | bytes 4194304 | tf_op jit(solution)/shard_map/while/body/eval_jaxpr/all_to_all | solution.py:130
  177.3 52.2 %all-to-all-start.1 = ((f32[2,1,2048,128]{3,1,0,2:T(1,128)}), f32[2,1,2048,128]{3,1,0,2:T(1,128)S(1)}, u32[]{:S(2)}, u32[]{:S(2)}) async-start(f32[2,1,2048,128]{3,1,0,2:T(1,128)} %copy.396), calls=%async_computation.1 | async-start | bytes 4194304 | tf_op jit(solution)/shard_map/while/body/eval_jaxpr/all_to_all | solution.py:130
  182.1 73.6 %all-gather.6.cloned.1.call-start = ((), (), s32[]{:S(2)}) async-start(), calls=%async_computation.3 | async-start | bytes 1572864 | tf_op jit(solution)/shard_map/while/body/eval_jaxpr/all_gather | solution.py:108
  235.2 3.9 copy-start.1
  282.0 52.2 %all-to-all-start = ((f32[2,1,128,2048]{2,1,0,3:T(1,128)}), f32[2,1,128,2048]{2,1,0,3:T(1,128)S(1)}, u32[]{:S(2)}, u32[]{:S(2)}) async-start(f32[2,1,128,2048]{2,1,0,3:T(1,128)} %pad_maximum_fusion.8), calls=%async_computation | async-start | bytes 4194304 | tf_op jit(solution)/shard_map/while/body/eval_jaxpr/all_to_all | solution.py:111
  334.2 1.3 copy-start
  346.7 2.5 copy-start.7
  347.9 1.5 copy-start.5
  348.0 1.8 copy-start.6
  382.0 4.9 copy-start.2
  382.0 52.4 %all-to-all-start.2 = ((f32[2,1,2048,128]{3,1,0,2:T(1,128)}), f32[2,1,2048,128]{3,1,0,2:T(1,128)}, u32[]{:S(2)}, u32[]{:S(2)}) async-start(f32[2,1,2048,128]{3,1,0,2:T(1,128)} %copy.403), calls=%async_computation.2 | async-start | bytes 4194304 | tf_op jit(solution)/shard_map/while/body/eval_jaxpr/all_to_all | solution.py:130
  434.4 52.2 %all-to-all-start.1 = ((f32[2,1,2048,128]{3,1,0,2:T(1,128)}), f32[2,1,2048,128]{3,1,0,2:T(1,128)S(1)}, u32[]{:S(2)}, u32[]{:S(2)}) async-start(f32[2,1,2048,128]{3,1,0,2:T(1,128)} %copy.396), calls=%async_computation.1 | async-start | bytes 4194304 | tf_op jit(solution)/shard_map/while/body/eval_jaxpr/all_to_all | solution.py:130
  439.2 73.8 %all-gather.6.cloned.1.call-start = ((), (), s32[]{:S(2)}) async-start(), calls=%async_computation.3 | async-start | bytes 1572864 | tf_op jit(solution)/shard_map/while/body/eval_jaxpr/all_gather | solution.py:108
  492.5 3.9 copy-start.1
  539.3 52.2 %all-to-all-start = ((f32[2,1,128,2048]{2,1,0,3:T(1,128)}), f32[2,1,128,2048]{2,1,0,3:T(1,128)S(1)}, u32[]{:S(2)}, u32[]{:S(2)}) async-start(f32[2,1,128,2048]{2,1,0,3:T(1,128)} %pad_maximum_fusion.8), calls=%async_computation | async-start | bytes 4194304 | tf_op jit(solution)/shard_map/while/body/eval_jaxpr/all_to_all | solution.py:111
  603.9 2.5 copy-start.7
  605.2 1.5 copy-start.5
  605.2 1.8 copy-start.6
  639.3 4.9 copy-start.2
  639.3 52.4 %all-to-all-start.2 = ((f32[2,1,2048,128]{3,1,0,2:T(1,128)}), f32[2,1,2048,128]{3,1,0,2:T(1,128)}, u32[]{:S(2)}, u32[]{:S(2)}) async-start(f32[2,1,2048,128]{3,1,0,2:T(1,128)} %copy.403), calls=%async_computation.2 | async-start | bytes 4194304 | tf_op jit(solution)/shard_map/while/body/eval_jaxpr/all_to_all | solution.py:130
  691.7 52.2 %all-to-all-start.1 = ((f32[2,1,2048,128]{3,1,0,2:T(1,128)}), f32[2,1,2048,128]{3,1,0,2:T(1,128)S(1)}, u32[]{:S(2)}, u32[]{:S(2)}) async-start(f32[2,1,2048,128]{3,1,0,2:T(1,128)} %copy.396), calls=%async_computation.1 | async-start | bytes 4194304 | tf_op jit(solution)/shard_map/while/body/eval_jaxpr/all_to_all | solution.py:130
  696.5 73.8 %all-gather.6.cloned.1.call-start = ((), (), s32[]{:S(2)}) async-start(), calls=%async_computation.3 | async-start | bytes 1572864 | tf_op jit(solution)/shard_map/while/body/eval_jaxpr/all_gather | solution.py:108
  749.6 3.9 copy-start.1
  782.5 1.3 copy-start.8
  (7 other events, 8.9 us)
Sparse Core Ops, SparseCore 0:
  184.5 21.7 all-gather.5
  441.5 21.7 all-gather.5
  698.8 21.7 all-gather.5
where the time goes:
time: 794 us; the launch traced here: 791 us
  waiting for transfers between devices  251 us (32%)
  matrix products  223 us (28%)
  local copies, waits for them, and re-layouts  167 us (21%)
  other arithmetic  75.2 us (9%)
  starting transfers between devices  45.2 us (6%)
  loops' own time  14.6 us (2%)
  between operations  14.1 us (2%)
    dot_general x144, matrix products, product(): return jnp.einsum(form, matrix, data, precision=lax.Precision.HIGHEST)  223 us
    all_to_all x6, waiting for transfers between devices, advance(): lax.all_to_all(shifted[branch], 'slab', split_axis=2, concat_axis=3, tile...  176 us
    all_to_all x3, waiting for transfers between devices, advance(): lax.all_to_all(jnp.stack((real, imag)), 'slab', split_axis=3, concat_axis...  74.5 us
    another operation x6, local copies, waits for them, and re-layouts, advance(): shifted.append(jnp.stack((back_real, back_imag)))  60.7 us
    another operation x6, other arithmetic, advance(): return jnp.stack((new_real, new_imag))  33.4 us
    select_n x3, other arithmetic, advance(): prop_imag = jnp.where(live, jnp.sin(angle), jnp.zeros_like(angle))  30.7 us
    all_to_all x12, local copies, waits for them, and re-layouts, advance(): lax.all_to_all(shifted[branch], 'slab', split_axis=2, concat_axis=3, tile...  29.5 us
    all_to_all x6, starting transfers between devices, advance(): lax.all_to_all(shifted[branch], 'slab', split_axis=2, concat_axis=3, tile...  29 us
  transfers between devices with their start and end apart: 12, of which 9 were waited for; matrix products, arithmetic and copies ran while one was open for 31% of the time, Pallas kernels for 0%

commit v1 on v0

--- a/solution.py
+++ b/solution.py
@@ -6,6 +6,29 @@
 
 two_pi = 2.0 * math.pi
 depth_step = 2.0
+
+
+def in_blocks(value, dim, size):
+    shape = value.shape
+    parts = value.reshape(*shape[:dim], size, shape[dim] // size, *shape[dim + 1 :])
+    return jnp.moveaxis(parts, dim, 0)
+
+
+def joined_along(tiles, dim):
+    lengths = list(tiles.shape[1:])
+    lengths[dim] *= tiles.shape[0]
+    return jnp.moveaxis(tiles, 0, dim).reshape(lengths)
+
+
+def rotated_exchange(x, axis, split_dim, concat_dim):
+    size, index = (lax.axis_size(axis), lax.axis_index(axis))
+    parts = in_blocks(x, split_dim, size)
+    outs = [parts[index]]
+    for hop in range(1, size):
+        sent = parts[(index + hop) % size]
+        outs.append(lax.ppermute(sent, axis, [(i, (i + hop) % size) for i in range(size)]))
+    parts = jnp.stack(outs)[(index - jnp.arange(size)) % size]
+    return joined_along(parts, concat_dim)
 
 
 def dft_matrix(length, sign):
@@ -107,9 +130,7 @@
         local_tile = lax.dynamic_index_in_dim(velocity, level, 0, keepdims=False)
         tile = lax.all_gather(local_tile, "freq", axis=1, tiled=True)
         real, imag = transform(field[0], field[1], False, -1)
-        spectrum = forward_x(
-            lax.all_to_all(jnp.stack((real, imag)), "slab", split_axis=3, concat_axis=2, tiled=True)
-        )
+        spectrum = forward_x(rotated_exchange(jnp.stack((real, imag)), "slab", 3, 2))
         slow_pair = lax.dynamic_index_in_dim(ref_slow, level, 0, keepdims=False)
         slowness = 1.0 / tile
         upper_weight = jnp.clip((slowness - slow_pair[0]) / (slow_pair[1] - slow_pair[0]), 0.0, 1.0)

time: 794 us -> 866 us (1.091)
  starting transfers between devices: 45.2 us -> 104 us
  local copies, waits for them, and re-layouts: 167 us -> 188 us
    all_to_all x3 -> x0, waiting for transfers between devices: 74.5 us -> none  [advance(): lax.all_to_all(jnp.stack((real, imag)), 'slab', split_axis=3, concat_axis...]
    ppermute x0 -> x45, waiting for transfers between devices: none -> 67.1 us  [rotated_exchange(): lax.ppermute(sent, axis, [(i, (i + hop) % size) for i in range(size)])]
    ppermute x0 -> x45, starting transfers between devices: none -> 62.9 us  [rotated_exchange(): lax.ppermute(sent, axis, [(i, (i + hop) % size) for i in range(size)])]
    all_to_all x3 -> x0, starting transfers between devices: 16.1 us -> none  [advance(): lax.all_to_all(jnp.stack((real, imag)), 'slab', split_axis=3, concat_axis...]
    while x60 -> x168, local copies, waits for them, and re-layouts: 8.15 us -> 21.9 us
    all_to_all x6, starting transfers between devices: 29 us -> 40.9 us  [advance(): lax.all_to_all(shifted[branch], 'slab', split_axis=2, concat_axis=3, tile...]
    gather x0 -> x6, local copies, waits for them, and re-layouts: none -> 10.8 us  [rotated_exchange(): parts = jnp.stack(outs)[(index - jnp.arange(size)) % size]]
    another operation x3 -> x0, other arithmetic: 9.91 us -> none  [advance(): jnp.stack((real, imag))]
  transfers between devices with their start and end apart: 12 -> 54, of which waited for: 9 -> 23; matrix products, arithmetic and copies ran while one was open for 31% -> 31% of each run, Pallas kernels for 0% -> 0%
where the time goes in v1:
time: 866 us; the launch traced here: 862 us
  waiting for transfers between devices  243 us (28%)
  matrix products  222 us (26%)
  local copies, waits for them, and re-layouts  188 us (22%)
  starting transfers between devices  104 us (12%)
  other arithmetic  74.8 us (9%)
  loops' own time  16.3 us (2%)
  between operations  14.1 us (2%)
    dot_general x144, matrix products, product(): return jnp.einsum(form, matrix, data, precision=lax.Precision.HIGHEST)  222 us
    all_to_all x6, waiting for transfers between devices, advance(): lax.all_to_all(shifted[branch], 'slab', split_axis=2, concat_axis=3, tile...  176 us
    ppermute x45, waiting for transfers between devices, rotated_exchange(): lax.ppermute(sent, axis, [(i, (i + hop) % size) for i in range(size)])  67.1 us
    ppermute x45, starting transfers between devices, rotated_exchange(): lax.ppermute(sent, axis, [(i, (i + hop) % size) for i in range(size)])  62.9 us
    another operation x6, local copies, waits for them, and re-layouts, advance(): shifted.append(jnp.stack((back_real, back_imag)))  60.7 us
    all_to_all x6, starting transfers between devices, advance(): lax.all_to_all(shifted[branch], 'slab', split_axis=2, concat_axis=3, tile...  40.9 us
    another operation x6, other arithmetic, advance(): return jnp.stack((new_real, new_imag))  33.6 us
    select_n x3, other arithmetic, advance(): prop_imag = jnp.where(live, jnp.sin(angle), jnp.zeros_like(angle))  30.8 us
  transfers between devices with their start and end apart: 54, of which 23 were waited for; matrix products, arithmetic and copies ran while one was open for 31% of the time, Pallas kernels for 0%

profile of v1, /device:TPU:11, one launch (start us, length us, event | category | flops | bytes accessed | tf_op | source)
XLA Modules:
  0.0 861.8 jit_solution(411018378671379160)
XLA Ops:
  8.1 845.6 %while.17 = (s32[]{:T(128)}, f32[2,1,128,2048]{3,2,1,0:T(8,128)S(1)}, f32[3,128,1024]{2,1,0:T(8,128)}, f32[3,2]{0,1:T(2,128)S(1)}, f32[1,1,1]{2,1,0:T(1,128)}, /...) while((s32[]{:T(128)}, ...), condition=%wide.region_1.2_spmd.clone, body=%wide.region_0.1_spmd.clone.sunk | while | flops 10909408256 | bytes 344036064 | solution.py:167
  31.1 10.3 %fusion.710 = (f32[2048,128]{1,0:T(8,128)}, f32[2048,128]{1,0:T(8,128)}, f32[2048,128]{1,0:T(8,128)S(1)}, f32[2048,128]{1,0:T(8,128)}) fusion(f32[128]{0:T(128)S(1)} %get-tuple-element.492, f32[2048]{0:T(1024)S(1)} %get-tuple-element.493, f32[]{:T(128)} %bitcast.754, f32[]{:T(128)} %bitcast.756), kind=kLoop, calls=%fused_computation.97.clone.1 | loop fusion | flops 3932160 | bytes 4203016 | tf_op jit(solution)/shard_map/while/body/eval_jaxpr/jit(_where)/select_n | solution.py:144
  62.6 9.7 %collective-permute-done.4 = f32[2,1,128,128]{3,2,0,1:T(8,128)S(1)} collective-permute-done((f32[2,1,128,128]{3,2,0,1:T(8,128)}, f32[2,1,128,128]{3,2,0,1:T(8,128)S(1)}, u32[]{:S(2)}, u32[]{:S(2)}) %collective-permute-start.4) | collective-permute-done | bytes 131104 | tf_op jit(solution)/shard_map/while/body/eval_jaxpr/ppermute | solution.py:29
  72.3 5.7 collective-permute-start.10
  85.5 9.5 %collective-permute-done.13 = f32[2,1,128,128]{3,2,0,1:T(8,128)S(1)} collective-permute-done((f32[2,1,128,128]{3,2,0,1:T(8,128)S(1)}, f32[2,1,128,128]{3,2,0,1:T(8,128)S(1)}, u32[]{:S(2)}, u32[]{:S(2)}) %collective-permute-start.13) | collective-permute-done | bytes 131104 | tf_op jit(solution)/shard_map/while/body/eval_jaxpr/ppermute | solution.py:29
  134.0 10.2 %copy.369 = f32[2,1,2048,128]{3,1,0,2:T(1,128)} copy(f32[2,1,2048,128]{3,2,1,0:T(8,128)S(1)} %pad_maximum_fusion.7) | data formatting | bytes 4194304 | tf_op jit(solution)/shard_map/while/body/eval_jaxpr/stack | solution.py:148
  144.2 6.6 all-to-all-start.1
  156.9 10.0 %copy.362 = f32[2,1,2048,128]{3,1,0,2:T(1,128)} copy(f32[2,1,2048,128]{3,2,1,0:T(8,128)S(1)} %pad_maximum_fusion.6) | data formatting | bytes 4194304 | tf_op jit(solution)/shard_map/while/body/eval_jaxpr/stack | solution.py:148
  166.9 31.4 %all-to-all-done.1 = f32[2,1,2048,128]{3,1,0,2:T(1,128)} async-done(((f32[2,1,2048,128]{3,1,0,2:T(1,128)}), f32[2,1,2048,128]{3,1,0,2:T(1,128)}, u32[]{:S(2)}, u32[]{:S(2)}) %all-to-all-start.1) | async-done | bytes 2097184 | tf_op jit(solution)/shard_map/while/body/eval_jaxpr/all_to_all | solution.py:151
  198.3 4.8 all-to-all-start
  223.5 27.0 %all-to-all-done = f32[2,1,2048,128]{3,1,0,2:T(1,128)S(1)} async-done(((f32[2,1,2048,128]{3,1,0,2:T(1,128)}), f32[2,1,2048,128]{3,1,0,2:T(1,128)S(1)}, u32[]{:S(2)}, u32[]{:S(2)}) %all-to-all-start) | async-done | bytes 2097184 | tf_op jit(solution)/shard_map/while/body/eval_jaxpr/all_to_all | solution.py:151
  276.7 11.0 %fusion.753 = (f32[1,1,128,2048]{3,2,1,0:T(8,128)S(1)}, f32[1,1,128,2048]{3,2,1,0:T(8,128)S(1)}) fusion(f32[16,8,16,128]{3,2,1,0:T(8,128)} %bitcast.812, f32[16,8,16,128]{3,2,1,0:T(8,128)S(1)} %bitcast.811, f32[16,8,16,128]{3,2,1,0:T(8,128)S(1)} %bitcast.810, f32[16,8,16,128]{3,2,1,0:T(8,128)S(1)} %bitcast.809, f32[]{:T(128)} %bitcast.781, ...), kind=kLoop, calls=%fused_computation.105.clone.1 | loop fusion | flops 6815744 | bytes 7340048 | tf_op jit(solution)/shard_map/while/body/eval_jaxpr/stack | solution.py:165
  311.2 10.3 %fusion.710 = (f32[2048,128]{1,0:T(8,128)}, f32[2048,128]{1,0:T(8,128)}, f32[2048,128]{1,0:T(8,128)S(1)}, f32[2048,128]{1,0:T(8,128)}) fusion(f32[128]{0:T(128)S(1)} %get-tuple-element.492, f32[2048]{0:T(1024)S(1)} %get-tuple-element.493, f32[]{:T(128)} %bitcast.754, f32[]{:T(128)} %bitcast.756), kind=kLoop, calls=%fused_computation.97.clone.1 | loop fusion | flops 3932160 | bytes 4203016 | tf_op jit(solution)/shard_map/while/body/eval_jaxpr/jit(_where)/select_n | solution.py:144
  341.9 10.2 %collective-permute-done.4 = f32[2,1,128,128]{3,2,0,1:T(8,128)S(1)} collective-permute-done((f32[2,1,128,128]{3,2,0,1:T(8,128)}, f32[2,1,128,128]{3,2,0,1:T(8,128)S(1)}, u32[]{:S(2)}, u32[]{:S(2)}) %collective-permute-start.4) | collective-permute-done | bytes 131104 | tf_op jit(solution)/shard_map/while/body/eval_jaxpr/ppermute | solution.py:29
  352.2 5.7 collective-permute-start.10
  364.2 8.4 collective-permute-done.13
  412.6 10.2 %copy.369 = f32[2,1,2048,128]{3,1,0,2:T(1,128)} copy(f32[2,1,2048,128]{3,2,1,0:T(8,128)S(1)} %pad_maximum_fusion.7) | data formatting | bytes 4194304 | tf_op jit(solution)/shard_map/while/body/eval_jaxpr/stack | solution.py:148
  422.7 10.0 %all-to-all-start.1 = ((f32[2,1,2048,128]{3,1,0,2:T(1,128)}), f32[2,1,2048,128]{3,1,0,2:T(1,128)}, u32[]{:S(2)}, u32[]{:S(2)}) async-start(f32[2,1,2048,128]{3,1,0,2:T(1,128)} %copy.369), calls=%async_computation.1 | async-start | bytes 4194304 | tf_op jit(solution)/shard_map/while/body/eval_jaxpr/all_to_all | solution.py:151
  438.9 10.0 %copy.362 = f32[2,1,2048,128]{3,1,0,2:T(1,128)} copy(f32[2,1,2048,128]{3,2,1,0:T(8,128)S(1)} %pad_maximum_fusion.6) | data formatting | bytes 4194304 | tf_op jit(solution)/shard_map/while/body/eval_jaxpr/stack | solution.py:148
  448.8 31.4 %all-to-all-done.1 = f32[2,1,2048,128]{3,1,0,2:T(1,128)} async-done(((f32[2,1,2048,128]{3,1,0,2:T(1,128)}), f32[2,1,2048,128]{3,1,0,2:T(1,128)}, u32[]{:S(2)}, u32[]{:S(2)}) %all-to-all-start.1) | async-done | bytes 2097184 | tf_op jit(solution)/shard_map/while/body/eval_jaxpr/all_to_all | solution.py:151
  505.2 27.2 %all-to-all-done = f32[2,1,2048,128]{3,1,0,2:T(1,128)S(1)} async-done(((f32[2,1,2048,128]{3,1,0,2:T(1,128)}), f32[2,1,2048,128]{3,1,0,2:T(1,128)S(1)}, u32[]{:S(2)}, u32[]{:S(2)}) %all-to-all-start) | async-done | bytes 2097184 | tf_op jit(solution)/shard_map/while/body/eval_jaxpr/all_to_all | solution.py:151
  558.8 11.0 %fusion.753 = (f32[1,1,128,2048]{3,2,1,0:T(8,128)S(1)}, f32[1,1,128,2048]{3,2,1,0:T(8,128)S(1)}) fusion(f32[16,8,16,128]{3,2,1,0:T(8,128)} %bitcast.812, f32[16,8,16,128]{3,2,1,0:T(8,128)S(1)} %bitcast.811, f32[16,8,16,128]{3,2,1,0:T(8,128)S(1)} %bitcast.810, f32[16,8,16,128]{3,2,1,0:T(8,128)S(1)} %bitcast.809, f32[]{:T(128)} %bitcast.781, ...), kind=kLoop, calls=%fused_computation.105.clone.1 | loop fusion | flops 6815744 | bytes 7340048 | tf_op jit(solution)/shard_map/while/body/eval_jaxpr/stack | solution.py:165
  593.3 10.3 %fusion.710 = (f32[2048,128]{1,0:T(8,128)}, f32[2048,128]{1,0:T(8,128)}, f32[2048,128]{1,0:T(8,128)S(1)}, f32[2048,128]{1,0:T(8,128)}) fusion(f32[128]{0:T(128)S(1)} %get-tuple-element.492, f32[2048]{0:T(1024)S(1)} %get-tuple-element.493, f32[]{:T(128)} %bitcast.754, f32[]{:T(128)} %bitcast.756), kind=kLoop, calls=%fused_computation.97.clone.1 | loop fusion | flops 3932160 | bytes 4203016 | tf_op jit(solution)/shard_map/while/body/eval_jaxpr/jit(_where)/select_n | solution.py:144
  624.1 10.2 %collective-permute-done.4 = f32[2,1,128,128]{3,2,0,1:T(8,128)S(1)} collective-permute-done((f32[2,1,128,128]{3,2,0,1:T(8,128)}, f32[2,1,128,128]{3,2,0,1:T(8,128)S(1)}, u32[]{:S(2)}, u32[]{:S(2)}) %collective-permute-start.4) | collective-permute-done | bytes 131104 | tf_op jit(solution)/shard_map/while/body/eval_jaxpr/ppermute | solution.py:29
  634.3 5.7 collective-permute-start.10
  646.4 8.3 collective-permute-done.13
  694.5 10.4 %copy.369 = f32[2,1,2048,128]{3,1,0,2:T(1,128)} copy(f32[2,1,2048,128]{3,2,1,0:T(8,128)S(1)} %pad_maximum_fusion.7) | data formatting | bytes 4194304 | tf_op jit(solution)/shard_map/while/body/eval_jaxpr/stack | solution.py:148
  704.9 10.0 %all-to-all-start.1 = ((f32[2,1,2048,128]{3,1,0,2:T(1,128)}), f32[2,1,2048,128]{3,1,0,2:T(1,128)}, u32[]{:S(2)}, u32[]{:S(2)}) async-start(f32[2,1,2048,128]{3,1,0,2:T(1,128)} %copy.369), calls=%async_computation.1 | async-start | bytes 4194304 | tf_op jit(solution)/shard_map/while/body/eval_jaxpr/all_to_all | solution.py:151
  721.0 10.0 %copy.362 = f32[2,1,2048,128]{3,1,0,2:T(1,128)} copy(f32[2,1,2048,128]{3,2,1,0:T(8,128)S(1)} %pad_maximum_fusion.6) | data formatting | bytes 4194304 | tf_op jit(solution)/shard_map/while/body/eval_jaxpr/stack | solution.py:148
  731.0 31.4 %all-to-all-done.1 = f32[2,1,2048,128]{3,1,0,2:T(1,128)} async-done(((f32[2,1,2048,128]{3,1,0,2:T(1,128)}), f32[2,1,2048,128]{3,1,0,2:T(1,128)}, u32[]{:S(2)}, u32[]{:S(2)}) %all-to-all-start.1) | async-done | bytes 2097184 | tf_op jit(solution)/shard_map/while/body/eval_jaxpr/all_to_all | solution.py:151
  787.3 27.3 %all-to-all-done = f32[2,1,2048,128]{3,1,0,2:T(1,128)S(1)} async-done(((f32[2,1,2048,128]{3,1,0,2:T(1,128)}), f32[2,1,2048,128]{3,1,0,2:T(1,128)S(1)}, u32[]{:S(2)}, u32[]{:S(2)}) %all-to-all-start) | async-done | bytes 2097184 | tf_op jit(solution)/shard_map/while/body/eval_jaxpr/all_to_all | solution.py:151
  841.0 11.0 %fusion.753 = (f32[1,1,128,2048]{3,2,1,0:T(8,128)S(1)}, f32[1,1,128,2048]{3,2,1,0:T(8,128)S(1)}) fusion(f32[16,8,16,128]{3,2,1,0:T(8,128)} %bitcast.812, f32[16,8,16,128]{3,2,1,0:T(8,128)S(1)} %bitcast.811, f32[16,8,16,128]{3,2,1,0:T(8,128)S(1)} %bitcast.810, f32[16,8,16,128]{3,2,1,0:T(8,128)S(1)} %bitcast.809, f32[]{:T(128)} %bitcast.781, ...), kind=kLoop, calls=%fused_computation.105.clone.1 | loop fusion | flops 6815744 | bytes 7340048 | tf_op jit(solution)/shard_map/while/body/eval_jaxpr/stack | solution.py:165
  (529 shorter events, 426.4 us)
Async XLA Ops:
  20.0 52.4 %collective-permute-start.5 = (f32[2,1,128,128]{3,2,0,1:T(8,128)}, f32[2,1,128,128]{3,2,0,1:T(8,128)}, u32[]{:S(2)}, u32[]{:S(2)}) collective-permute-start(f32[2,1,128,128]{3,2,0,1:T(8,128)} %get-tuple-element.399), channel_id=1, source_target_pairs={{0,6},{1,7},{2,8},{3,9},{4,10},{5,11},{6,12},{7,13},{8,14},{9,15},... | collective-permute-start | bytes 393224 | tf_op jit(solution)/shard_map/while/body/eval_jaxpr/ppermute | solution.py:29
  23.1 28.7 %collective-permute-start = (f32[2,1,128,128]{3,2,0,1:T(8,128)}, f32[2,1,128,128]{3,2,0,1:T(8,128)}, u32[]{:S(2)}, u32[]{:S(2)}) collective-permute-start(f32[2,1,128,128]{3,2,0,1:T(8,128)} %get-tuple-element.394), channel_id=1, source_target_pairs={{0,1},{1,2},{2,3},{3,4},{4,5},{5,6},{6,7},{7,8},{8,9},{9,10},{10,1... | collective-permute-start | bytes 393224 | tf_op jit(solution)/shard_map/while/body/eval_jaxpr/ppermute | solution.py:29
  25.2 31.4 %collective-permute-start.1 = (f32[2,1,128,128]{3,2,0,1:T(8,128)}, f32[2,1,128,128]{3,2,0,1:T(8,128)}, u32[]{:S(2)}, u32[]{:S(2)}) collective-permute-start(f32[2,1,128,128]{3,2,0,1:T(8,128)} %get-tuple-element.395), channel_id=1, source_target_pairs={{0,2},{1,3},{2,4},{3,5},{4,6},{5,7},{6,8},{7,9},{8,10},{9,11},{10,... | collective-permute-start | bytes 393224 | tf_op jit(solution)/shard_map/while/body/eval_jaxpr/ppermute | solution.py:29
  25.2 33.9 %collective-permute-start.2 = (f32[2,1,128,128]{3,2,0,1:T(8,128)}, f32[2,1,128,128]{3,2,0,1:T(8,128)}, u32[]{:S(2)}, u32[]{:S(2)}) collective-permute-start(f32[2,1,128,128]{3,2,0,1:T(8,128)} %get-tuple-element.396), channel_id=1, source_target_pairs={{0,3},{1,4},{2,5},{3,6},{4,7},{5,8},{6,9},{7,10},{8,11},{9,12},{10... | collective-permute-start | bytes 393224 | tf_op jit(solution)/shard_map/while/body/eval_jaxpr/ppermute | solution.py:29
  25.4 34.8 %collective-permute-start.3 = (f32[2,1,128,128]{3,2,0,1:T(8,128)}, f32[2,1,128,128]{3,2,0,1:T(8,128)}, u32[]{:S(2)}, u32[]{:S(2)}) collective-permute-start(f32[2,1,128,128]{3,2,0,1:T(8,128)} %get-tuple-element.397), channel_id=1, source_target_pairs={{0,4},{1,5},{2,6},{3,7},{4,8},{5,9},{6,10},{7,11},{8,12},{9,13},{1... | collective-permute-start | bytes 393224 | tf_op jit(solution)/shard_map/while/body/eval_jaxpr/ppermute | solution.py:29
  51.9 20.4 %collective-permute-start.4 = (f32[2,1,128,128]{3,2,0,1:T(8,128)}, f32[2,1,128,128]{3,2,0,1:T(8,128)S(1)}, u32[]{:S(2)}, u32[]{:S(2)}) collective-permute-start(f32[2,1,128,128]{3,2,0,1:T(8,128)} %get-tuple-element.398), channel_id=1, source_target_pairs={{0,5},{1,6},{2,7},{3,8},{4,9},{5,10},{6,11},{7,12},{8,13},{9,14},{... | collective-permute-start | bytes 393224 | tf_op jit(solution)/shard_map/while/body/eval_jaxpr/ppermute | solution.py:29
  56.6 22.3 %collective-permute-start.6 = (f32[2,1,128,128]{3,2,0,1:T(8,128)S(1)}, f32[2,1,128,128]{3,2,0,1:T(8,128)S(1)}, u32[]{:S(2)}, u32[]{:S(2)}) collective-permute-start(f32[2,1,128,128]{3,2,0,1:T(8,128)S(1)} %copy-done.13), channel_id=1, source_target_pairs={{0,7},{1,8},{2,9},{3,10},{4,11},{5,12},{6,13},{7,14},{8,15},{9,0},... | collective-permute-start | bytes 393224 | tf_op jit(solution)/shard_map/while/body/eval_jaxpr/ppermute | solution.py:29
  144.2 54.1 %all-to-all-start.1 = ((f32[2,1,2048,128]{3,1,0,2:T(1,128)}), f32[2,1,2048,128]{3,1,0,2:T(1,128)}, u32[]{:S(2)}, u32[]{:S(2)}) async-start(f32[2,1,2048,128]{3,1,0,2:T(1,128)} %copy.369), calls=%async_computation.1 | async-start | bytes 4194304 | tf_op jit(solution)/shard_map/while/body/eval_jaxpr/all_to_all | solution.py:151
  198.3 52.2 %all-to-all-start = ((f32[2,1,2048,128]{3,1,0,2:T(1,128)}), f32[2,1,2048,128]{3,1,0,2:T(1,128)S(1)}, u32[]{:S(2)}, u32[]{:S(2)}) async-start(f32[2,1,2048,128]{3,1,0,2:T(1,128)} %copy.362), calls=%async_computation | async-start | bytes 4194304 | tf_op jit(solution)/shard_map/while/body/eval_jaxpr/all_to_all | solution.py:151
  203.1 73.6 %all-gather.6.cloned.1.call-start = ((), (), s32[]{:S(2)}) async-start(), calls=%async_computation.2 | async-start | bytes 1572864 | tf_op jit(solution)/shard_map/while/body/eval_jaxpr/all_gather | solution.py:131
  300.6 51.5 %collective-permute-start.5 = (f32[2,1,128,128]{3,2,0,1:T(8,128)}, f32[2,1,128,128]{3,2,0,1:T(8,128)}, u32[]{:S(2)}, u32[]{:S(2)}) collective-permute-start(f32[2,1,128,128]{3,2,0,1:T(8,128)} %get-tuple-element.399), channel_id=1, source_target_pairs={{0,6},{1,7},{2,8},{3,9},{4,10},{5,11},{6,12},{7,13},{8,14},{9,15},... | collective-permute-start | bytes 393224 | tf_op jit(solution)/shard_map/while/body/eval_jaxpr/ppermute | solution.py:29
  301.5 30.4 %collective-permute-start = (f32[2,1,128,128]{3,2,0,1:T(8,128)}, f32[2,1,128,128]{3,2,0,1:T(8,128)}, u32[]{:S(2)}, u32[]{:S(2)}) collective-permute-start(f32[2,1,128,128]{3,2,0,1:T(8,128)} %get-tuple-element.394), channel_id=1, source_target_pairs={{0,1},{1,2},{2,3},{3,4},{4,5},{5,6},{6,7},{7,8},{8,9},{9,10},{10,1... | collective-permute-start | bytes 393224 | tf_op jit(solution)/shard_map/while/body/eval_jaxpr/ppermute | solution.py:29
  304.1 31.3 %collective-permute-start.1 = (f32[2,1,128,128]{3,2,0,1:T(8,128)}, f32[2,1,128,128]{3,2,0,1:T(8,128)}, u32[]{:S(2)}, u32[]{:S(2)}) collective-permute-start(f32[2,1,128,128]{3,2,0,1:T(8,128)} %get-tuple-element.395), channel_id=1, source_target_pairs={{0,2},{1,3},{2,4},{3,5},{4,6},{5,7},{6,8},{7,9},{8,10},{9,11},{10,... | collective-permute-start | bytes 393224 | tf_op jit(solution)/shard_map/while/body/eval_jaxpr/ppermute | solution.py:29
  304.1 33.8 %collective-permute-start.2 = (f32[2,1,128,128]{3,2,0,1:T(8,128)}, f32[2,1,128,128]{3,2,0,1:T(8,128)}, u32[]{:S(2)}, u32[]{:S(2)}) collective-permute-start(f32[2,1,128,128]{3,2,0,1:T(8,128)} %get-tuple-element.396), channel_id=1, source_target_pairs={{0,3},{1,4},{2,5},{3,6},{4,7},{5,8},{6,9},{7,10},{8,11},{9,12},{10... | collective-permute-start | bytes 393224 | tf_op jit(solution)/shard_map/while/body/eval_jaxpr/ppermute | solution.py:29
  304.1 36.0 %collective-permute-start.3 = (f32[2,1,128,128]{3,2,0,1:T(8,128)}, f32[2,1,128,128]{3,2,0,1:T(8,128)}, u32[]{:S(2)}, u32[]{:S(2)}) collective-permute-start(f32[2,1,128,128]{3,2,0,1:T(8,128)} %get-tuple-element.397), channel_id=1, source_target_pairs={{0,4},{1,5},{2,6},{3,7},{4,8},{5,9},{6,10},{7,11},{8,12},{9,13},{1... | collective-permute-start | bytes 393224 | tf_op jit(solution)/shard_map/while/body/eval_jaxpr/ppermute | solution.py:29
  331.9 20.2 %collective-permute-start.4 = (f32[2,1,128,128]{3,2,0,1:T(8,128)}, f32[2,1,128,128]{3,2,0,1:T(8,128)S(1)}, u32[]{:S(2)}, u32[]{:S(2)}) collective-permute-start(f32[2,1,128,128]{3,2,0,1:T(8,128)} %get-tuple-element.398), channel_id=1, source_target_pairs={{0,5},{1,6},{2,7},{3,8},{4,9},{5,10},{6,11},{7,12},{8,13},{9,14},{... | collective-permute-start | bytes 393224 | tf_op jit(solution)/shard_map/while/body/eval_jaxpr/ppermute | solution.py:29
  335.4 23.4 %collective-permute-start.6 = (f32[2,1,128,128]{3,2,0,1:T(8,128)S(1)}, f32[2,1,128,128]{3,2,0,1:T(8,128)S(1)}, u32[]{:S(2)}, u32[]{:S(2)}) collective-permute-start(f32[2,1,128,128]{3,2,0,1:T(8,128)S(1)} %copy-done.13), channel_id=1, source_target_pairs={{0,7},{1,8},{2,9},{3,10},{4,11},{5,12},{6,13},{7,14},{8,15},{9,0},... | collective-permute-start | bytes 393224 | tf_op jit(solution)/shard_map/while/body/eval_jaxpr/ppermute | solution.py:29
  337.9 20.9 %collective-permute-start.7 = (f32[2,1,128,128]{3,2,0,1:T(8,128)S(1)}, f32[2,1,128,128]{3,2,0,1:T(8,128)S(1)}, u32[]{:S(2)}, u32[]{:S(2)}) collective-permute-start(f32[2,1,128,128]{3,2,0,1:T(8,128)S(1)} %copy-done.12), channel_id=1, source_target_pairs={{0,8},{1,9},{2,10},{3,11},{4,12},{5,13},{6,14},{7,15},{8,0},{9,1},... | collective-permute-start | bytes 393224 | tf_op jit(solution)/shard_map/while/body/eval_jaxpr/ppermute | solution.py:29
  422.7 57.5 %all-to-all-start.1 = ((f32[2,1,2048,128]{3,1,0,2:T(1,128)}), f32[2,1,2048,128]{3,1,0,2:T(1,128)}, u32[]{:S(2)}, u32[]{:S(2)}) async-start(f32[2,1,2048,128]{3,1,0,2:T(1,128)} %copy.369), calls=%async_computation.1 | async-start | bytes 4194304 | tf_op jit(solution)/shard_map/while/body/eval_jaxpr/all_to_all | solution.py:151
  480.3 52.2 %all-to-all-start = ((f32[2,1,2048,128]{3,1,0,2:T(1,128)}), f32[2,1,2048,128]{3,1,0,2:T(1,128)S(1)}, u32[]{:S(2)}, u32[]{:S(2)}) async-start(f32[2,1,2048,128]{3,1,0,2:T(1,128)} %copy.362), calls=%async_computation | async-start | bytes 4194304 | tf_op jit(solution)/shard_map/while/body/eval_jaxpr/all_to_all | solution.py:151
  485.0 73.8 %all-gather.6.cloned.1.call-start = ((), (), s32[]{:S(2)}) async-start(), calls=%async_computation.2 | async-start | bytes 1572864 | tf_op jit(solution)/shard_map/while/body/eval_jaxpr/all_gather | solution.py:131
  582.6 51.8 %collective-permute-start.5 = (f32[2,1,128,128]{3,2,0,1:T(8,128)}, f32[2,1,128,128]{3,2,0,1:T(8,128)}, u32[]{:S(2)}, u32[]{:S(2)}) collective-permute-start(f32[2,1,128,128]{3,2,0,1:T(8,128)} %get-tuple-element.399), channel_id=1, source_target_pairs={{0,6},{1,7},{2,8},{3,9},{4,10},{5,11},{6,12},{7,13},{8,14},{9,15},... | collective-permute-start | bytes 393224 | tf_op jit(solution)/shard_map/while/body/eval_jaxpr/ppermute | solution.py:29
  583.5 30.6 %collective-permute-start = (f32[2,1,128,128]{3,2,0,1:T(8,128)}, f32[2,1,128,128]{3,2,0,1:T(8,128)}, u32[]{:S(2)}, u32[]{:S(2)}) collective-permute-start(f32[2,1,128,128]{3,2,0,1:T(8,128)} %get-tuple-element.394), channel_id=1, source_target_pairs={{0,1},{1,2},{2,3},{3,4},{4,5},{5,6},{6,7},{7,8},{8,9},{9,10},{10,1... | collective-permute-start | bytes 393224 | tf_op jit(solution)/shard_map/while/body/eval_jaxpr/ppermute | solution.py:29
  586.1 31.5 %collective-permute-start.1 = (f32[2,1,128,128]{3,2,0,1:T(8,128)}, f32[2,1,128,128]{3,2,0,1:T(8,128)}, u32[]{:S(2)}, u32[]{:S(2)}) collective-permute-start(f32[2,1,128,128]{3,2,0,1:T(8,128)} %get-tuple-element.395), channel_id=1, source_target_pairs={{0,2},{1,3},{2,4},{3,5},{4,6},{5,7},{6,8},{7,9},{8,10},{9,11},{10,... | collective-permute-start | bytes 393224 | tf_op jit(solution)/shard_map/while/body/eval_jaxpr/ppermute | solution.py:29
  586.1 34.0 %collective-permute-start.2 = (f32[2,1,128,128]{3,2,0,1:T(8,128)}, f32[2,1,128,128]{3,2,0,1:T(8,128)}, u32[]{:S(2)}, u32[]{:S(2)}) collective-permute-start(f32[2,1,128,128]{3,2,0,1:T(8,128)} %get-tuple-element.396), channel_id=1, source_target_pairs={{0,3},{1,4},{2,5},{3,6},{4,7},{5,8},{6,9},{7,10},{8,11},{9,12},{10... | collective-permute-start | bytes 393224 | tf_op jit(solution)/shard_map/while/body/eval_jaxpr/ppermute | solution.py:29
  586.1 36.2 %collective-permute-start.3 = (f32[2,1,128,128]{3,2,0,1:T(8,128)}, f32[2,1,128,128]{3,2,0,1:T(8,128)}, u32[]{:S(2)}, u32[]{:S(2)}) collective-permute-start(f32[2,1,128,128]{3,2,0,1:T(8,128)} %get-tuple-element.397), channel_id=1, source_target_pairs={{0,4},{1,5},{2,6},{3,7},{4,8},{5,9},{6,10},{7,11},{8,12},{9,13},{1... | collective-permute-start | bytes 393224 | tf_op jit(solution)/shard_map/while/body/eval_jaxpr/ppermute | solution.py:29
  614.1 20.2 %collective-permute-start.4 = (f32[2,1,128,128]{3,2,0,1:T(8,128)}, f32[2,1,128,128]{3,2,0,1:T(8,128)S(1)}, u32[]{:S(2)}, u32[]{:S(2)}) collective-permute-start(f32[2,1,128,128]{3,2,0,1:T(8,128)} %get-tuple-element.398), channel_id=1, source_target_pairs={{0,5},{1,6},{2,7},{3,8},{4,9},{5,10},{6,11},{7,12},{8,13},{9,14},{... | collective-permute-start | bytes 393224 | tf_op jit(solution)/shard_map/while/body/eval_jaxpr/ppermute | solution.py:29
  617.6 23.4 %collective-permute-start.6 = (f32[2,1,128,128]{3,2,0,1:T(8,128)S(1)}, f32[2,1,128,128]{3,2,0,1:T(8,128)S(1)}, u32[]{:S(2)}, u32[]{:S(2)}) collective-permute-start(f32[2,1,128,128]{3,2,0,1:T(8,128)S(1)} %copy-done.13), channel_id=1, source_target_pairs={{0,7},{1,8},{2,9},{3,10},{4,11},{5,12},{6,13},{7,14},{8,15},{9,0},... | collective-permute-start | bytes 393224 | tf_op jit(solution)/shard_map/while/body/eval_jaxpr/ppermute | solution.py:29
  620.1 20.9 %collective-permute-start.7 = (f32[2,1,128,128]{3,2,0,1:T(8,128)S(1)}, f32[2,1,128,128]{3,2,0,1:T(8,128)S(1)}, u32[]{:S(2)}, u32[]{:S(2)}) collective-permute-start(f32[2,1,128,128]{3,2,0,1:T(8,128)S(1)} %copy-done.12), channel_id=1, source_target_pairs={{0,8},{1,9},{2,10},{3,11},{4,12},{5,13},{6,14},{7,15},{8,0},{9,1},... | collective-permute-start | bytes 393224 | tf_op jit(solution)/shard_map/while/body/eval_jaxpr/ppermute | solution.py:29
  704.9 57.5 %all-to-all-start.1 = ((f32[2,1,2048,128]{3,1,0,2:T(1,128)}), f32[2,1,2048,128]{3,1,0,2:T(1,128)}, u32[]{:S(2)}, u32[]{:S(2)}) async-start(f32[2,1,2048,128]{3,1,0,2:T(1,128)} %copy.369), calls=%async_computation.1 | async-start | bytes 4194304 | tf_op jit(solution)/shard_map/while/body/eval_jaxpr/all_to_all | solution.py:151
  762.4 52.2 %all-to-all-start = ((f32[2,1,2048,128]{3,1,0,2:T(1,128)}), f32[2,1,2048,128]{3,1,0,2:T(1,128)S(1)}, u32[]{:S(2)}, u32[]{:S(2)}) async-start(f32[2,1,2048,128]{3,1,0,2:T(1,128)} %copy.362), calls=%async_computation | async-start | bytes 4194304 | tf_op jit(solution)/shard_map/while/body/eval_jaxpr/all_to_all | solution.py:151
  767.2 73.8 %all-gather.6.cloned.1.call-start = ((), (), s32[]{:S(2)}) async-start(), calls=%async_computation.2 | async-start | bytes 1572864 | tf_op jit(solution)/shard_map/while/body/eval_jaxpr/all_gather | solution.py:131
  (82 other events, 639.1 us)
Sparse Core Ops, SparseCore 0:
  205.5 21.7 all-gather.5
  487.4 21.7 all-gather.5
  769.5 21.7 all-gather.5
